TPU v7x, 32 devices: a whole 2x2x4 slice. The times are simulated.
32 devices in a mesh: dp: 8 (over z, x), seq: 4 (over y, core).
Axes of the slice: x: 2, y: 2, z: 4, core: 2. Of those that a mesh axis runs over, the one named last changes fastest.
Arguments:
- inputs: bfloat16 [8, 2048, 768], P('dp', 'seq'), may hold values from -2.5 to 2.5
- cotangent: bfloat16 [8, 2048, 768], P('dp', 'seq'), may hold values from -6 to 6
- qkv_weight: float32 [768, 2304], P('seq', 'dp'), may hold values from -0.21875 to 0.21875
- qkv_first: float32 [768, 2304], P('seq', 'dp'), may hold values from -128 to 128
- qkv_second: float32 [768, 2304], P('seq', 'dp'), may hold values from 491.52 to 4096
- out_weight: float32 [768, 768], P('seq', 'dp'), may hold values from -2.5 to 2.5
- out_first: float32 [768, 768], P('seq', 'dp'), may hold values from -13.57645 to 13.57645
- out_second: float32 [768, 768], P('seq', 'dp'), may hold values from 5.76 to 46.08
- fc_weight: float32 [768, 3072], P('seq', 'dp'), may hold values from -0.21875 to 0.21875
- fc_first: float32 [768, 3072], P('seq', 'dp'), may hold values from -46.08 to 46.08
- fc_second: float32 [768, 3072], P('seq', 'dp'), may hold values from 65.536 to 524.288
- proj_weight: float32 [3072, 768], P('seq', 'dp'), may hold values from -0.109375 to 0.109375
- proj_first: float32 [3072, 768], P('seq', 'dp'), may hold values from -97.28 to 97.28
- proj_second: float32 [3072, 768], P('seq', 'dp'), may hold values from 294.912 to 2359.296
- vectors: float32 [12, 768], P('seq', 'dp'), may hold values from -0.4 to 1.4, as said below
- vector_first: float32 [12, 768], P('seq', 'dp'), may hold values from -128 to 128
- vector_second: float32 [12, 768], P('seq', 'dp'), may hold values from 327.68 to 4096
Outputs:
- outputs: bfloat16 [8, 2048, 768], P('dp', 'seq')
- input_grad: bfloat16 [8, 2048, 768], P('dp', 'seq')
- qkv_first_new: float32 [768, 2304], P('seq', 'dp')
- qkv_second_new: float32 [768, 2304], P('seq', 'dp')
- qkv_updated: float32 [768, 2304], P('seq', 'dp')
- qkv_lowered: bfloat16 [768, 2304], P('seq', 'dp')
- out_first_new: float32 [768, 768], P('seq', 'dp')
- out_second_new: float32 [768, 768], P('seq', 'dp')
- out_updated: float32 [768, 768], P('seq', 'dp')
- out_lowered: bfloat16 [768, 768], P('seq', 'dp')
- fc_first_new: float32 [768, 3072], P('seq', 'dp')
- fc_second_new: float32 [768, 3072], P('seq', 'dp')
- fc_updated: float32 [768, 3072], P('seq', 'dp')
- fc_lowered: bfloat16 [768, 3072], P('seq', 'dp')
- proj_first_new: float32 [3072, 768], P('seq', 'dp')
- proj_second_new: float32 [3072, 768], P('seq', 'dp')
- proj_updated: float32 [3072, 768], P('seq', 'dp')
- proj_lowered: bfloat16 [3072, 768], P('seq', 'dp')
- vector_first_new: float32 [12, 768], P('seq', 'dp')
- vector_second_new: float32 [12, 768], P('seq', 'dp')
- vector_updated: float32 [12, 768], P('seq', 'dp')
- vector_lowered: bfloat16 [12, 768], P('seq', 'dp')
Inputs may be any that keep to these rules, and one draw needn't show every extreme that they name: `vectors`: rows 0 and 5 are LayerNorm gains near one, the other rows are biases of order a tenth.
All inputs are finite; a program needn't handle non-finite values.
Results may differ from a plain program's by a relative error of at most 0.018.
Values may be sent and summed in bfloat16 or wider, within the bound.
No kernel may reach another device: no remote copies, remote signals or barrier semaphores. Data moves between devices by JAX's collectives and lax.ppermute only.
A program may use at most 192 MiB of HBM per device.

v0:
```python
import jax
import jax.numpy as jnp
from jax import lax
from jax.sharding import PartitionSpec as P

D = 768
HEADS = 12
HEAD_DIM = 64
FF = 3072
DEPTH = 12
LEN = 2048
STEP = 10
beta_one = 0.5
beta_two = 0.5
matrix_decay = 0.1


def layer_norm(values, gain, shift):
    centre = values - jnp.mean(values, -1, keepdims=True)
    spread = jnp.mean(centre * centre, -1, keepdims=True)
    return centre * lax.rsqrt(spread + 1e-05) * gain + shift


def gelu_tanh(values):
    return jax.nn.gelu(values, approximate=True)


def adam_update(master, first, second, grad, rate, decay):
    first_new = beta_one * first + (1.0 - beta_one) * grad
    second_new = beta_two * second + (1.0 - beta_two) * grad * grad
    fix_one = 1.0 - beta_one**STEP
    fix_two = 1.0 - beta_two**STEP
    direction = first_new / fix_one / (jnp.sqrt(second_new / fix_two) + 1e-08)
    updated = master - rate * (direction + decay * master)
    return (first_new, second_new, updated, updated.astype(jnp.bfloat16))


def attend_forward(query_all, key_all, value_all):
    head_count, seq_len, head_width = query_all.shape
    block_len = min(512, seq_len)
    block_count = seq_len // block_len
    score_scale = head_width ** (-0.5)
    key_pos = jnp.arange(seq_len)[None, None, :]

    def one_block(block_index):
        block_start = block_index * block_len
        query_blk = lax.dynamic_slice_in_dim(query_all, block_start, block_len, 1)
        scores = (
            jnp.einsum("gqd,gkd->gqk", query_blk, key_all, preferred_element_type=jnp.float32)
            * score_scale
        )
        query_pos = block_start + jnp.arange(block_len)[None, :, None]
        scores = jnp.where(key_pos <= query_pos, scores, -1e30)
        row_max = jnp.max(scores, -1, keepdims=True)
        exponent = jnp.exp(scores - row_max)
        row_total = jnp.sum(exponent, -1, keepdims=True)
        attn_probs = (exponent / row_total).astype(jnp.bfloat16)
        block_out = jnp.einsum(
            "gqk,gkd->gqd", attn_probs, value_all, preferred_element_type=jnp.float32
        )
        return (block_out.astype(jnp.bfloat16), row_max + jnp.log(row_total))

    block_out, log_total = lax.map(one_block, jnp.arange(block_count))
    block_out = block_out.transpose(1, 0, 2, 3).reshape(head_count, seq_len, head_width)
    log_total = log_total.transpose(1, 0, 2, 3).reshape(head_count, seq_len, 1)
    return (block_out, log_total)


def attend_backward(query_all, key_all, value_all, grad_all, log_total):
    head_count, seq_len, head_width = query_all.shape
    block_len = min(512, seq_len)
    block_count = seq_len // block_len
    score_scale = head_width ** (-0.5)
    key_pos = jnp.arange(seq_len)[None, None, :]

    def one_block(carry, block_index):
        key_grad, value_grad = carry
        block_start = block_index * block_len
        query_blk = lax.dynamic_slice_in_dim(query_all, block_start, block_len, 1)
        grad_blk = lax.dynamic_slice_in_dim(grad_all, block_start, block_len, 1)
        total_blk = lax.dynamic_slice_in_dim(log_total, block_start, block_len, 1)
        scores = (
            jnp.einsum("gqd,gkd->gqk", query_blk, key_all, preferred_element_type=jnp.float32)
            * score_scale
        )
        query_pos = block_start + jnp.arange(block_len)[None, :, None]
        scores = jnp.where(key_pos <= query_pos, scores, -1e30)
        attn_probs = jnp.exp(scores - total_blk)
        grad_probs = jnp.einsum(
            "gqd,gkd->gqk", grad_blk, value_all, preferred_element_type=jnp.float32
        )
        inner = jnp.sum(attn_probs * grad_probs, -1, keepdims=True)
        grad_scores = (attn_probs * (grad_probs - inner)).astype(jnp.bfloat16)
        query_grad = (
            jnp.einsum("gqk,gkd->gqd", grad_scores, key_all, preferred_element_type=jnp.float32)
            * score_scale
        )
        key_grad = (
            key_grad
            + jnp.einsum("gqk,gqd->gkd", grad_scores, query_blk, preferred_element_type=jnp.float32)
            * score_scale
        )
        value_grad = value_grad + jnp.einsum(
            "gqk,gqd->gkd",
            attn_probs.astype(jnp.bfloat16),
            grad_blk,
            preferred_element_type=jnp.float32,
        )
        return ((key_grad, value_grad), query_grad)

    empty = jnp.zeros((head_count, seq_len, head_width), jnp.float32)
    (key_grad, value_grad), query_grad = lax.scan(
        one_block, (empty, empty), jnp.arange(block_count)
    )
    query_grad = query_grad.transpose(1, 0, 2, 3).reshape(head_count, seq_len, head_width)
    return jnp.stack([query_grad, key_grad, value_grad]).astype(jnp.bfloat16)


def token_sum(left, right):
    return jnp.einsum("ti,to->io", left, right, preferred_element_type=jnp.float32)


def back_product(grad_rows, weight):
    return jnp.einsum("to,io->ti", grad_rows, weight, preferred_element_type=jnp.float32)


def local(
    inputs,
    cotangent,
    qkv_weight,
    qkv_first,
    qkv_second,
    out_weight,
    out_first,
    out_second,
    fc_weight,
    fc_first,
    fc_second,
    proj_weight,
    proj_first,
    proj_second,
    vectors,
    vector_first,
    vector_second,
):
    branch = DEPTH ** (-0.5)
    seq_parts = lax.axis_size("seq")
    seq_count, part_len, features = inputs.shape
    tok_rows = seq_count * part_len
    seq_len = part_len * seq_parts
    head_groups = HEADS // seq_parts
    group_width = head_groups * HEAD_DIM
    low_qkv = qkv_weight.astype(jnp.bfloat16)
    low_out = out_weight.astype(jnp.bfloat16)
    low_fc = fc_weight.astype(jnp.bfloat16)
    low_proj = proj_weight.astype(jnp.bfloat16)
    low_vec = vectors.astype(jnp.bfloat16)
    wide_qkv, wide_out, wide_fc, wide_proj, wide_vec = (
        lax.all_gather(low_qkv, "dp", axis=1, tiled=True),
        lax.all_gather(low_out, "dp", axis=1, tiled=True),
        lax.all_gather(low_fc, "dp", axis=1, tiled=True),
        lax.all_gather(low_proj, "dp", axis=1, tiled=True),
        lax.all_gather(low_vec, "dp", axis=1, tiled=True),
    )
    w_qkv, w_out, w_fc, w_proj, w_vec = (
        lax.all_gather(wide_qkv, "seq", axis=0, tiled=True),
        lax.all_gather(wide_out, "seq", axis=0, tiled=True),
        lax.all_gather(wide_fc, "seq", axis=0, tiled=True),
        lax.all_gather(wide_proj, "seq", axis=0, tiled=True),
        lax.all_gather(wide_vec, "seq", axis=0, tiled=True),
    )
    vec_used = w_vec.astype(jnp.float32)
    tokens_in = inputs.astype(jnp.float32).reshape(tok_rows, features)
    h_one = layer_norm(tokens_in, vec_used[0], vec_used[1]).astype(jnp.bfloat16)
    qkv_bias = jnp.concatenate([vec_used[2], jnp.zeros_like(vec_used[2]), vec_used[3]])
    qkv_rows = (jnp.dot(h_one, w_qkv, preferred_element_type=jnp.float32) + qkv_bias).astype(
        jnp.bfloat16
    )
    outgoing = qkv_rows.reshape(seq_count, part_len, 3, seq_parts, group_width)
    arrived = lax.all_to_all(outgoing, "seq", split_axis=3, concat_axis=1, tiled=True)
    heads_all = arrived.reshape(seq_count, seq_len, 3, head_groups, HEAD_DIM).transpose(
        2, 0, 3, 1, 4
    )
    attn_heads, log_total = lax.map(
        lambda items: attend_forward(items[0], items[1], items[2]),
        (heads_all[0], heads_all[1], heads_all[2]),
    )
    leaving = attn_heads.transpose(0, 2, 1, 3).reshape(seq_count, seq_len, 1, group_width)
    returned = lax.all_to_all(leaving, "seq", split_axis=1, concat_axis=2, tiled=True)
    attn_rows = returned.reshape(tok_rows, features)
    attn_out = jnp.dot(attn_rows, w_out, preferred_element_type=jnp.float32) + vec_used[4]
    middle = tokens_in + branch * attn_out
    h_two = layer_norm(middle, vec_used[5], vec_used[6]).astype(jnp.bfloat16)
    hidden = jnp.dot(h_two, w_fc, preferred_element_type=jnp.float32) + vec_used[8:].reshape(-1)
    active = gelu_tanh(hidden).astype(jnp.bfloat16)
    mlp_out = jnp.dot(active, w_proj, preferred_element_type=jnp.float32) + vec_used[7]
    outputs = (middle + branch * mlp_out).astype(jnp.bfloat16).reshape(inputs.shape)
    back_qkv, back_out, back_fc, back_proj = (w_qkv, w_out, w_fc, w_proj)
    grad_out = cotangent.astype(jnp.float32).reshape(tok_rows, features)
    grad_mlp = (branch * grad_out).astype(jnp.bfloat16)
    grad_proj = token_sum(active, grad_mlp)
    grad_proj_bias = jnp.sum(grad_mlp.astype(jnp.float32), 0)
    grad_active = back_product(grad_mlp, back_proj)
    gelu_value, gelu_pull = jax.vjp(gelu_tanh, hidden)
    grad_hidden = gelu_pull(grad_active)[0].astype(jnp.bfloat16)
    grad_fc = token_sum(h_two, grad_hidden)
    grad_fc_bias = jnp.sum(grad_hidden.astype(jnp.float32), 0)
    grad_norm_two = back_product(grad_hidden, back_fc)
    norm_value, norm_pull = jax.vjp(layer_norm, middle, vec_used[5], vec_used[6])
    grad_mid_norm, grad_gain_two, grad_shift_two = norm_pull(grad_norm_two)
    grad_middle = grad_out + grad_mid_norm
    grad_attn_out = (branch * grad_middle).astype(jnp.bfloat16)
    grad_outproj = token_sum(attn_rows, grad_attn_out)
    grad_out_bias = jnp.sum(grad_attn_out.astype(jnp.float32), 0)
    grad_attn = back_product(grad_attn_out, back_out).astype(jnp.bfloat16)
    sending = grad_attn.reshape(seq_count, part_len, seq_parts, group_width)
    grad_arrived = lax.all_to_all(sending, "seq", split_axis=2, concat_axis=1, tiled=True)
    grad_heads = grad_arrived.reshape(seq_count, seq_len, head_groups, HEAD_DIM).transpose(
        0, 2, 1, 3
    )
    grad_qkv_heads = lax.map(
        lambda items: attend_backward(items[0], items[1], items[2], items[3], items[4]),
        (heads_all[0], heads_all[1], heads_all[2], grad_heads, log_total),
    )
    back_leaving = grad_qkv_heads.transpose(0, 3, 1, 2, 4).reshape(
        seq_count, seq_len, 3, 1, group_width
    )
    back_rows = lax.all_to_all(back_leaving, "seq", split_axis=1, concat_axis=3, tiled=True)
    grad_qkv = back_rows.reshape(tok_rows, 3 * features)
    grad_qkv_weight = token_sum(h_one, grad_qkv)
    qkv_sums = jnp.sum(grad_qkv.astype(jnp.float32), 0)
    grad_norm_one = back_product(grad_qkv, back_qkv)
    first_value, first_pull = jax.vjp(layer_norm, tokens_in, vec_used[0], vec_used[1])
    grad_in_norm, grad_gain_one, grad_shift_one = first_pull(grad_norm_one)
    input_grad = (grad_middle + grad_in_norm).astype(jnp.bfloat16).reshape(inputs.shape)
    grad_vec = jnp.concatenate(
        [
            jnp.stack(
                [
                    grad_gain_one,
                    grad_shift_one,
                    qkv_sums[:features],
                    qkv_sums[2 * features :],
                    grad_out_bias,
                    grad_gain_two,
                    grad_shift_two,
                    grad_proj_bias,
                ]
            ),
            grad_fc_bias.reshape(-1, features),
        ],
        0,
    )
    part_qkv, part_out, part_fc, part_proj, part_vec = (
        lax.psum_scatter(grad_qkv_weight, "dp", scatter_dimension=1, tiled=True),
        lax.psum_scatter(grad_outproj, "dp", scatter_dimension=1, tiled=True),
        lax.psum_scatter(grad_fc, "dp", scatter_dimension=1, tiled=True),
        lax.psum_scatter(grad_proj, "dp", scatter_dimension=1, tiled=True),
        lax.psum_scatter(grad_vec, "dp", scatter_dimension=1, tiled=True),
    )
    sum_qkv, sum_out, sum_fc, sum_proj, sum_vec = (
        lax.psum_scatter(
            part_qkv.astype(jnp.bfloat16), "seq", scatter_dimension=0, tiled=True
        ).astype(jnp.float32),
        lax.psum_scatter(
            part_out.astype(jnp.bfloat16), "seq", scatter_dimension=0, tiled=True
        ).astype(jnp.float32),
        lax.psum_scatter(
            part_fc.astype(jnp.bfloat16), "seq", scatter_dimension=0, tiled=True
        ).astype(jnp.float32),
        lax.psum_scatter(
            part_proj.astype(jnp.bfloat16), "seq", scatter_dimension=0, tiled=True
        ).astype(jnp.float32),
        lax.psum_scatter(
            part_vec.astype(jnp.bfloat16), "seq", scatter_dimension=0, tiled=True
        ).astype(jnp.float32),
    )
    qkv_new = adam_update(qkv_weight, qkv_first, qkv_second, sum_qkv, D ** (-0.5), matrix_decay)
    out_new = adam_update(
        out_weight, out_first, out_second, sum_out, max(1, 16 * D // LEN) ** (-0.5), matrix_decay
    )
    fc_new = adam_update(fc_weight, fc_first, fc_second, sum_fc, D ** (-0.5), matrix_decay)
    proj_new = adam_update(
        proj_weight, proj_first, proj_second, sum_proj, FF ** (-0.5), matrix_decay
    )
    vec_new = adam_update(vectors, vector_first, vector_second, sum_vec, 0.5, 0.0)
    return (
        outputs,
        input_grad,
        qkv_new[0],
        qkv_new[1],
        qkv_new[2],
        qkv_new[3],
        out_new[0],
        out_new[1],
        out_new[2],
        out_new[3],
        fc_new[0],
        fc_new[1],
        fc_new[2],
        fc_new[3],
        proj_new[0],
        proj_new[1],
        proj_new[2],
        proj_new[3],
        vec_new[0],
        vec_new[1],
        vec_new[2],
        vec_new[3],
    )


def solution(mesh):
    return jax.shard_map(
        local,
        mesh=mesh,
        in_specs=(
            P("dp", "seq", None),
            P("dp", "seq", None),
            P("seq", "dp"),
            P("seq", "dp"),
            P("seq", "dp"),
            P("seq", "dp"),
            P("seq", "dp"),
            P("seq", "dp"),
            P("seq", "dp"),
            P("seq", "dp"),
            P("seq", "dp"),
            P("seq", "dp"),
            P("seq", "dp"),
            P("seq", "dp"),
            P("seq", "dp"),
            P("seq", "dp"),
            P("seq", "dp"),
        ),
        out_specs=(
            P("dp", "seq", None),
            P("dp", "seq", None),
            P("seq", "dp"),
            P("seq", "dp"),
            P("seq", "dp"),
            P("seq", "dp"),
            P("seq", "dp"),
            P("seq", "dp"),
            P("seq", "dp"),
            P("seq", "dp"),
            P("seq", "dp"),
            P("seq", "dp"),
            P("seq", "dp"),
            P("seq", "dp"),
            P("seq", "dp"),
            P("seq", "dp"),
            P("seq", "dp"),
            P("seq", "dp"),
            P("seq", "dp"),
            P("seq", "dp"),
            P("seq", "dp"),
            P("seq", "dp"),
        ),
        check_vma=False,
    )
```

profile of v0, /device:TPU:0, one launch (start us, length us, event | category | flops | bytes accessed | tf_op | source)
XLA Modules:
  0.0 1290.6 jit_solution(14631618596200599561)
XLA Ops:
  9.1 35.4 %all_gather.32 = bf16[192,2304]{0,1:T(8,128)(2,1)S(1)} all-gather(bf16[192,288]{0,1:T(8,128)(2,1)S(1)} %convert_element_type.140), channel_id=1, replica_groups=mesh['dp'=8,'seq'=4] {'dp'}, dimensions={1}, use_global_device_ids=true | all-gather | bytes 995328 | tf_op jit(solution)/shard_map/all_gather | solution.py:159
  47.4 31.1 %all_gather.34 = bf16[192,768]{0,1:T(8,128)(2,1)S(1)} all-gather(bf16[192,96]{0,1:T(8,128)(2,1)S(1)} %convert_element_type.142), channel_id=1, replica_groups=mesh['dp'=8,'seq'=4] {'dp'}, dimensions={1}, use_global_device_ids=true | all-gather | bytes 331776 | tf_op jit(solution)/shard_map/all_gather | solution.py:160
  79.4 20.3 %all-gather = bf16[8,96,3]{1,2,0:T(4,128)(2,1)S(1)} all-gather(bf16[1,96,3]{1,2,0:T(4,128)(2,1)S(1)} %convert_bitcast_fusion.4), channel_id=1, replica_groups=mesh['dp'=8,'seq'=4] {'dp'}, dimensions={0}, use_global_device_ids=true | all-gather | bytes 5184 | tf_op jit(solution)/shard_map/all_gather | solution.py:163
  121.8 34.2 %all-to-all-done = bf16[1,512,3,4,192]{1,4,2,0,3:T(8,128)(2,1)S(1)} async-done(((bf16[1,512,3,4,192]{1,4,2,0,3:T(8,128)(2,1)}), bf16[1,512,3,4,192]{1,4,2,0,3:T(8,128)(2,1)S(1)}, u32[]{:S(2)}, u32[]{:S(2)}) %all-to-all-start) | async-done | bytes 2359328 | tf_op jit(solution)/shard_map/all_to_all | solution.py:180
  167.1 87.8 %while.46 = (s32[]{:T(128)}, bf16[4,3,512,64]{2,3,1,0:T(8,128)(2,1)}, f32[4,3,512,1]{2,1,3,0:T(4,128)S(1)}, s32[4]{0:T(128)S(1)}, bf16[3,2048,64]{1,2,0:T(8,128)...) while((s32[]{:T(128)}, ...), condition=%wide.region_5.6_spmd.clone, body=%wide.region_2.5_spmd.clone.sunk | while | flops 844200960 | bytes 43968700 | solution.py:63
  181.8 7.3 fusion.155
  203.8 7.3 fusion.155
  225.7 7.3 fusion.155
  247.6 7.3 fusion.155
  264.5 12.7 reduce.19
  283.2 11.5 all-to-all-done.1
  326.1 159.5 %reduce-scatter.24.cloned.1.call-done = f32[3072,96]{0,1:T(8,128)} async-done(((f32[3072,768]{0,1:T(8,128)}), f32[3072,96]{0,1:T(8,128)}) %reduce-scatter.24.cloned.1.call-update) | async-done | bytes 1179664 | tf_op jit(solution)/shard_map/reduce_scatter | solution.py:258
  487.9 21.9 %reduce-scatter.26.cloned.1.call-done = bf16[768,96]{0,1:T(8,128)(2,1)} async-done(((bf16[3072,96]{0,1:T(8,128)(2,1)}), bf16[768,96]{0,1:T(8,128)(2,1)}) %reduce-scatter.26.cloned.1.call-update) | async-done | bytes 147472 | tf_op jit(solution)/shard_map/reduce_scatter | solution.py:271
  512.4 41.2 %all-gather.17.cloned.1.call-done = bf16[768,768]{0,1:T(8,128)(2,1)} async-done(((bf16[768,96]{0,1:T(8,128)(2,1)}), bf16[768,768]{0,1:T(8,128)(2,1)}) %all-gather.17.cloned.1.call-update) | async-done | bytes 1179664 | tf_op jit(solution)/shard_map/all_gather | solution.py:162
  553.6 37.8 %all-gather.19.cloned.1.call-done = bf16[3072,768]{0,1:T(8,128)(2,1)} async-done(((bf16[768,768]{0,1:T(8,128)(2,1)}), bf16[3072,768]{0,1:T(8,128)(2,1)}) %all-gather.19.cloned.1.call-update) | async-done | bytes 4718608 | tf_op jit(solution)/shard_map/all_gather | solution.py:169
  591.5 10.6 convert_reduce_fusion
  622.1 7.8 all-to-all-done.2
  634.3 138.9 %while.47 = (s32[]{:T(128)}, f32[3,2048,64]{1,2,0:T(8,128)}, f32[3,2048,64]{1,2,0:T(8,128)}, bf16[4,3,512,64]{2,3,1,0:T(8,128)(2,1)}, s32[4]{0:T(128)S(1)}, /*in...) while((s32[]{:T(128)}, f32[3,2048,64]{1,2,0:T(8,128)}, ...), condition=%wide.region_12.13_spmd.clone, body=%wide.region_10.12_spmd.clone.sunk | while | flops 2063563776 | bytes 219593376 | solution.py:112
  639.9 7.4 multiply_reduce_fusion.5
  674.3 7.3 multiply_reduce_fusion.5
  709.1 7.3 multiply_reduce_fusion.5
  743.8 7.3 multiply_reduce_fusion.5
  782.4 53.9 %all_to_all.60 = bf16[1,2048,3,1,192]{4,2,3,0,1:T(4,128)(2,1)} all-to-all(bf16[1,2048,3,1,192]{4,2,3,0,1:T(4,128)(2,1)} %copy.188), channel_id=1, replica_groups=mesh['dp'=8,'seq'=4] {'seq'}, dimensions={1} | all-to-all | bytes 4718592 | tf_op jit(solution)/shard_map/all_to_all | solution.py:228
  836.2 7.2 copy.209
  851.4 9.0 fusion.93
  875.9 104.0 %reduce-scatter.16.cloned.1.call-done = f32[768,288]{0,1:T(8,128)} async-done(((f32[768,2304]{0,1:T(8,128)}), f32[768,288]{0,1:T(8,128)}) %reduce-scatter.16.cloned.1.call-update) | async-done | bytes 884752 | tf_op jit(solution)/shard_map/reduce_scatter | solution.py:255
  982.4 9.1 fusion.63
  991.5 155.0 %reduce-scatter.20.cloned.1.call-done = f32[768,384]{1,0:T(8,128)} async-done(((f32[768,3072]{1,0:T(8,128)}), f32[768,384]{1,0:T(8,128)}) %reduce-scatter.20.cloned.1.call-update) | async-done | bytes 1179664 | tf_op jit(solution)/shard_map/reduce_scatter | solution.py:257
  1151.8 58.6 %reduce-scatter.32.cloned.1.call-done = f32[96,12]{1,0:T(8,128)} async-done(((f32[768,12]{1,0:T(8,128)}), f32[96,12]{1,0:T(8,128)}) %reduce-scatter.32.cloned.1.call-update) | async-done | bytes 4624
  1218.3 14.1 %reduce-scatter.30.cloned.1.call-done = bf16[192,96]{1,0:T(8,128)(2,1)} async-done(((bf16[768,96]{1,0:T(8,128)(2,1)}), bf16[192,96]{1,0:T(8,128)(2,1)}) %reduce-scatter.30.cloned.1.call-update) | async-done | bytes 36880
  1237.3 19.7 %reduce-scatter.28.cloned.1.call-done = bf16[192,288]{1,0:T(8,128)(2,1)} async-done(((bf16[768,288]{1,0:T(8,128)(2,1)}), bf16[192,288]{1,0:T(8,128)(2,1)}) %reduce-scatter.28.cloned.1.call-update) | async-done | bytes 110608
  1262.7 18.9 %reduce-scatter.22.cloned.1.call-done = bf16[192,384]{1,0:T(8,128)(2,1)} async-done(((bf16[768,384]{1,0:T(8,128)(2,1)}), bf16[192,384]{1,0:T(8,128)(2,1)}) %reduce-scatter.22.cloned.1.call-update) | async-done | bytes 147472 | tf_op jit(solution)/shard_map/reduce_scatter | solution.py:268
  (451 shorter events, 335.9 us)
Async XLA Ops:
  7.2 99.6 %all-gather.9.cloned.1.call-start = ((), (), s32[]{:S(2)}) async-start(), calls=%async_computation.13 | async-start | bytes 4423680 | tf_op jit(solution)/shard_map/all_gather | solution.py:166
  44.5 61.1 %copy-start.9 = (bf16[1,512,768]{2,1,0:T(8,128)(2,1)S(1)}, bf16[1,512,768]{2,1,0:T(8,128)(2,1)}, u32[]{:S(2)}) copy-start(bf16[1,512,768]{2,1,0:T(8,128)(2,1)} %param.21) | copy-start | bytes 2359300
  45.8 75.4 %all-gather.13.cloned.1.call-start = ((), (), s32[]{:S(2)}) async-start(), calls=%async_computation.15 | async-start | bytes 1327104 | tf_op jit(solution)/shard_map/all_gather | solution.py:161
  46.6 261.9 %all-gather.11.cloned.1.call-start = ((), (), s32[]{:S(2)}) async-start(), calls=%async_computation.14 | async-start | bytes 1474560 | tf_op jit(solution)/shard_map/all_gather | solution.py:167
  117.5 38.4 %all-to-all-start = ((bf16[1,512,3,4,192]{1,4,2,0,3:T(8,128)(2,1)}), bf16[1,512,3,4,192]{1,4,2,0,3:T(8,128)(2,1)S(1)}, u32[]{:S(2)}, u32[]{:S(2)}) async-start(bf16[1,512,3,4,192]{1,4,2,0,3:T(8,128)(2,1)} %copy.176), calls=%async_computation | async-start | bytes 4718592 | tf_op jit(solution)/shard_map/all_to_all | solution.py:180
  121.2 191.3 %all-gather.15.cloned.1.call-start = ((), (), s32[]{:S(2)}) async-start(), calls=%async_computation.16 | async-start | bytes 5898240 | tf_op jit(solution)/shard_map/all_gather | solution.py:168
  279.6 15.1 %all-to-all-start.1 = ((bf16[4,2,49152]{2,1,0:T(2,128)(2,1)}), bf16[4,2,49152]{2,1,0:T(2,128)(2,1)S(1)}, u32[]{:S(2)}, u32[]{:S(2)}) async-start(bf16[4,2,49152]{2,1,0:T(2,128)(2,1)} %reshape.401), calls=%async_computation.1 | async-start | bytes 1572864 | tf_op jit(solution)/shard_map/all_to_all | solution.py:189
  283.1 202.6 %reduce-scatter.24.cloned.1.call-start = ((), (), s32[]{:S(2)}) async-start(), calls=%async_computation.23 | async-start | bytes 10616832 | tf_op jit(solution)/shard_map/reduce_scatter | solution.py:258
  283.1 308.3 %copy-start.55 = (f32[3072]{0:T(1024)}, f32[3072]{0:T(1024)S(1)}, u32[]{:S(2)}) copy-start(f32[3072]{0:T(1024)S(1)} %add.276) | copy-start | bytes 36868
  311.0 298.1 %copy-start.46 = (f32[512]{0:T(512)}, f32[512]{0:T(512)S(1)}, u32[]{:S(2)}) copy-start(f32[512]{0:T(512)S(1)} %broadcast_multiply_fusion) | copy-start | bytes 6148
  312.5 296.7 %copy-start.58 = (f32[512]{0:T(512)}, f32[512]{0:T(512)S(1)}, u32[]{:S(2)}) copy-start(f32[512]{0:T(512)S(1)} %fusion.89) | copy-start | bytes 6148
  326.1 183.7 %reduce-scatter.26.cloned.1.call-start = ((), (), s32[]{:S(2)}) async-start(), calls=%async_computation.24 | async-start | bytes 737280 | tf_op jit(solution)/shard_map/reduce_scatter | solution.py:271
  487.8 65.8 %all-gather.17.cloned.1.call-start = ((), (), s32[]{:S(2)}) async-start(), calls=%async_computation.17 | async-start | bytes 1327104 | tf_op jit(solution)/shard_map/all_gather | solution.py:162
  512.4 79.1 %all-gather.19.cloned.1.call-start = ((), (), s32[]{:S(2)}) async-start(), calls=%async_computation.18 | async-start | bytes 5898240 | tf_op jit(solution)/shard_map/all_gather | solution.py:169
  614.9 15.1 %all-to-all-start.2 = ((bf16[1,512,4,192]{1,3,0,2:T(8,128)(2,1)}), bf16[1,512,4,192]{1,3,0,2:T(8,128)(2,1)S(1)}, u32[]{:S(2)}, u32[]{:S(2)}) async-start(bf16[1,512,4,192]{1,3,0,2:T(8,128)(2,1)} %bitcast.202), calls=%async_computation.2 | async-start | bytes 1572864 | tf_op jit(solution)/shard_map/all_to_all | solution.py:217
  618.4 251.2 %reduce-scatter.18.cloned.1.call-start = ((), (), s32[]{:S(2)}) async-start(), calls=%async_computation.20 | async-start | bytes 2654208 | tf_op jit(solution)/shard_map/reduce_scatter | solution.py:256
  622.1 357.9 %reduce-scatter.16.cloned.1.call-start = ((), (), s32[]{:S(2)}) async-start(), calls=%async_computation.19 | async-start | bytes 7962624 | tf_op jit(solution)/shard_map/reduce_scatter | solution.py:255
  850.7 295.8 %reduce-scatter.20.cloned.1.call-start = ((), (), s32[]{:S(2)}) async-start(), calls=%async_computation.21 | async-start | bytes 10616832 | tf_op jit(solution)/shard_map/reduce_scatter | solution.py:257
  860.4 350.0 %reduce-scatter.32.cloned.1.call-start = ((), (), s32[]{:S(2)}) async-start(), calls=%async_computation.27 | async-start | bytes 442368
  869.5 362.9 %reduce-scatter.30.cloned.1.call-start = ((), (), s32[]{:S(2)}) async-start(), calls=%async_computation.26 | async-start | bytes 245760
  871.4 110.9 %copy-start.16 = (f32[512,768]{1,0:T(8,128)S(1)}, f32[512,768]{1,0:T(8,128)}, u32[]{:S(2)}) copy-start(f32[512,768]{1,0:T(8,128)} %copy-done.14) | copy-start | bytes 4718596
  871.4 110.9 %copy-start.56 = (f32[3072]{0:T(1024)S(1)}, f32[3072]{0:T(1024)}, u32[]{:S(2)}) copy-start(f32[3072]{0:T(1024)} %copy-done.55) | copy-start | bytes 36868
  871.4 110.9 %copy-start.61 = (f32[768]{0:T(1024)S(1)}, f32[768]{0:T(1024)}, u32[]{:S(2)}) copy-start(f32[768]{0:T(1024)} %get-tuple-element.359) | copy-start | bytes 9220
  871.4 385.6 %reduce-scatter.28.cloned.1.call-start = ((), (), s32[]{:S(2)}) async-start(), calls=%async_computation.25 | async-start | bytes 737280
  982.3 299.3 %reduce-scatter.22.cloned.1.call-start = ((), (), s32[]{:S(2)}) async-start(), calls=%async_computation.22 | async-start | bytes 737280 | tf_op jit(solution)/shard_map/reduce_scatter | solution.py:268
  991.4 157.3 %copy-start.8 = (f32[512,768]{1,0:T(8,128)S(1)}, f32[512,768]{1,0:T(8,128)}, u32[]{:S(2)}) copy-start(f32[512,768]{1,0:T(8,128)} %copy-done.7) | copy-start | bytes 4718596
  991.4 157.3 %copy-start.19 = (bf16[1,512,768]{2,1,0:T(8,128)(2,1)S(1)}, bf16[1,512,768]{2,1,0:T(8,128)(2,1)}, u32[]{:S(2)}) copy-start(bf16[1,512,768]{2,1,0:T(8,128)(2,1)} %param.22) | copy-start | bytes 2359300
  1148.7 84.6 %copy-start.29 = (f32[192,96]{0,1:T(8,128)S(1)}, f32[192,96]{0,1:T(8,128)}, u32[]{:S(2)}) copy-start(f32[192,96]{0,1:T(8,128)} %copy-done.28) | copy-start | bytes 221188
  1148.7 109.3 %copy-start.22 = (f32[192,288]{0,1:T(8,128)S(1)}, f32[192,288]{0,1:T(8,128)}, u32[]{:S(2)}) copy-start(f32[192,288]{0,1:T(8,128)} %copy-done.21) | copy-start | bytes 663556
  1235.8 45.8 %copy-start.27 = (f32[192,384]{1,0:T(8,128)S(1)}, f32[192,384]{1,0:T(8,128)}, u32[]{:S(2)}) copy-start(f32[192,384]{1,0:T(8,128)} %param.29) | copy-start | bytes 884740
  1235.8 45.8 %copy-start.34 = (f32[192,384]{1,0:T(8,128)S(1)}, f32[192,384]{1,0:T(8,128)}, u32[]{:S(2)}) copy-start(f32[192,384]{1,0:T(8,128)} %param.31) | copy-start | bytes 884740
  1235.8 45.8 %copy-start.35 = (f32[192,384]{1,0:T(8,128)S(1)}, f32[192,384]{1,0:T(8,128)}, u32[]{:S(2)}) copy-start(f32[192,384]{1,0:T(8,128)} %param.30) | copy-start | bytes 884740
  (104 other events, 538.4 us)
Sparse Core Ops, SparseCore 0:
  45.9 31.3 all-gather.8
  79.9 40.8 all-gather.12
  123.0 22.7 all-gather.10
  147.2 37.4 all-gather.14
  326.2 159.4 reduce-scatter.23
  488.6 21.1 reduce-scatter.25
  512.5 41.0 all-gather.16
  555.2 36.2 all-gather.18
  622.7 70.4 reduce-scatter.17
  850.8 129.1 reduce-scatter.15
  984.0 162.4 reduce-scatter.19
  1149.9 60.4 reduce-scatter.31
  1213.6 18.7 reduce-scatter.29
  1234.9 22.0 reduce-scatter.27
  1259.5 22.0 reduce-scatter.21
where the time goes:
time: 1300 us; the launch traced here: 1290 us
  waiting for transfers between devices  685 us (53%)
  matrix products  217 us (17%)
  blocking collectives  151 us (12%)
  local copies, waits for them, and re-layouts  102 us (8%)
  other arithmetic  100 us (8%)
  between operations  15.9 us (1%)
    reduce_scatter x1, waiting for transfers between devices, local(): lax.psum_scatter(grad_proj, 'dp', scatter_dimension=1, tiled=True)  160 us
    reduce_scatter x1, waiting for transfers between devices, local(): lax.psum_scatter(grad_fc, 'dp', scatter_dimension=1, tiled=True)  155 us
    reduce_scatter x1, waiting for transfers between devices, local(): lax.psum_scatter(grad_qkv_weight, 'dp', scatter_dimension=1, tiled=True)  104 us
    unnamed x18, waiting for transfers between devices  93.2 us
    all_to_all x1, blocking collectives, local(): lax.all_to_all(back_leaving, 'seq', split_axis=1, concat_axis=3, tiled=True)  53.9 us
    all_gather x1, waiting for transfers between devices, local(): lax.all_gather(low_proj, 'dp', axis=1, tiled=True)  41.2 us
    all_gather x1, waiting for transfers between devices, local(): lax.all_gather(wide_proj, 'seq', axis=0, tiled=True)  37.8 us
    all_gather x1, blocking collectives, local(): lax.all_gather(low_qkv, 'dp', axis=1, tiled=True)  35.4 us
  transfers between devices with their start and end apart: 18, of which 13 were waited for; matrix products, arithmetic and copies ran while one was open for 28% of the time, Pallas kernels for 0%

commit v1 on v0

--- a/solution.py
+++ b/solution.py
@@ -13,6 +13,18 @@
 beta_one = 0.5
 beta_two = 0.5
 matrix_decay = 0.1
+
+
+def collect(value, axis, dim):
+    ways, here = (lax.axis_size(axis), lax.axis_index(axis))
+    grown, reach = (value, 1)
+    while reach < ways:
+        theirs = lax.ppermute(grown, axis, [(d, d ^ reach) for d in range(ways)])
+        mine_first = jnp.concatenate([grown, theirs], axis=dim)
+        theirs_first = jnp.concatenate([theirs, grown], axis=dim)
+        grown = jnp.where(here & reach == 0, mine_first, theirs_first)
+        reach = 2 * reach
+    return grown
 
 
 def layer_norm(values, gain, shift):
@@ -166,7 +178,7 @@
         lax.all_gather(wide_qkv, "seq", axis=0, tiled=True),
         lax.all_gather(wide_out, "seq", axis=0, tiled=True),
         lax.all_gather(wide_fc, "seq", axis=0, tiled=True),
-        lax.all_gather(wide_proj, "seq", axis=0, tiled=True),
+        collect(wide_proj, "seq", 0),
         lax.all_gather(wide_vec, "seq", axis=0, tiled=True),
     )
     vec_used = w_vec.astype(jnp.float32)

time: 1300 us -> 1320 us (1.015)
  waiting for transfers between devices: 685 us -> 699 us
    ppermute x0 -> x2, waiting for transfers between devices: none -> 55.3 us  [collect(): theirs = lax.ppermute(grown, axis, [(d, d ^ reach) for d in range(ways)])]
    all_gather x1 -> x0, waiting for transfers between devices: 37.8 us -> none  [local(): lax.all_gather(wide_proj, 'seq', axis=0, tiled=True)]
    unnamed x18 -> x17, waiting for transfers between devices: 93.2 us -> 93.2 us
  transfers between devices with their start and end apart: 18 -> 19, of which waited for: 13 -> 14; matrix products, arithmetic and copies ran while one was open for 28% -> 28% of each run, Pallas kernels for 0% -> 0%
where the time goes in v1:
time: 1320 us; the launch traced here: 1310 us
  waiting for transfers between devices  699 us (53%)
  matrix products  221 us (17%)
  blocking collectives  151 us (11%)
  other arithmetic  104 us (8%)
  local copies, waits for them, and re-layouts  102 us (8%)
  between operations  15.7 us (1%)
    reduce_scatter x1, waiting for transfers between devices, local(): lax.psum_scatter(grad_proj, 'dp', scatter_dimension=1, tiled=True)  160 us
    reduce_scatter x1, waiting for transfers between devices, local(): lax.psum_scatter(grad_fc, 'dp', scatter_dimension=1, tiled=True)  153 us
    reduce_scatter x1, waiting for transfers between devices, local(): lax.psum_scatter(grad_qkv_weight, 'dp', scatter_dimension=1, tiled=True)  102 us
    unnamed x17, waiting for transfers between devices  93.2 us
    ppermute x2, waiting for transfers between devices, collect(): theirs = lax.ppermute(grown, axis, [(d, d ^ reach) for d in range(ways)])  55.3 us
    all_to_all x1, blocking collectives, local(): lax.all_to_all(back_leaving, 'seq', split_axis=1, concat_axis=3, tiled=True)  53.9 us
    all_gather x1, waiting for transfers between devices, local(): lax.all_gather(low_proj, 'dp', axis=1, tiled=True)  41.3 us
    all_gather x1, blocking collectives, local(): lax.all_gather(low_qkv, 'dp', axis=1, tiled=True)  35.4 us
  transfers between devices with their start and end apart: 19, of which 14 were waited for; matrix products, arithmetic and copies ran while one was open for 28% of the time, Pallas kernels for 0%

profile of v1, /device:TPU:0, one launch (start us, length us, event | category | flops | bytes accessed | tf_op | source)
XLA Modules:
  0.0 1313.4 jit_solution(2982157891912748607)
XLA Ops:
  9.1 35.4 %all_gather.29 = bf16[192,2304]{0,1:T(8,128)(2,1)S(1)} all-gather(bf16[192,288]{0,1:T(8,128)(2,1)S(1)} %convert_element_type.140), channel_id=1, replica_groups=mesh['dp'=8,'seq'=4] {'dp'}, dimensions={1}, use_global_device_ids=true | all-gather | bytes 995328 | tf_op jit(solution)/shard_map/all_gather | solution.py:171
  47.4 31.1 %all_gather.31 = bf16[192,768]{0,1:T(8,128)(2,1)S(1)} all-gather(bf16[192,96]{0,1:T(8,128)(2,1)S(1)} %convert_element_type.142), channel_id=1, replica_groups=mesh['dp'=8,'seq'=4] {'dp'}, dimensions={1}, use_global_device_ids=true | all-gather | bytes 331776 | tf_op jit(solution)/shard_map/all_gather | solution.py:172
  79.4 20.3 %all-gather = bf16[8,96,3]{1,2,0:T(4,128)(2,1)S(1)} all-gather(bf16[1,96,3]{1,2,0:T(4,128)(2,1)S(1)} %convert_bitcast_fusion.4), channel_id=1, replica_groups=mesh['dp'=8,'seq'=4] {'dp'}, dimensions={0}, use_global_device_ids=true | all-gather | bytes 5184 | tf_op jit(solution)/shard_map/all_gather | solution.py:175
  121.7 34.2 %all-to-all-done = bf16[1,512,3,4,192]{1,4,2,0,3:T(8,128)(2,1)S(1)} async-done(((bf16[1,512,3,4,192]{1,4,2,0,3:T(8,128)(2,1)}), bf16[1,512,3,4,192]{1,4,2,0,3:T(8,128)(2,1)S(1)}, u32[]{:S(2)}, u32[]{:S(2)}) %all-to-all-start) | async-done | bytes 2359328 | tf_op jit(solution)/shard_map/all_to_all | solution.py:192
  167.2 87.8 %while.46 = (s32[]{:T(128)}, bf16[4,3,512,64]{2,3,1,0:T(8,128)(2,1)}, f32[4,3,512,1]{2,1,3,0:T(4,128)S(1)}, s32[4]{0:T(128)S(1)}, bf16[3,2048,64]{1,2,0:T(8,128)...) while((s32[]{:T(128)}, ...), condition=%wide.region_5.6_spmd.clone, body=%wide.region_2.5_spmd.clone.sunk | while | flops 844200960 | bytes 43968700 | solution.py:75
  181.9 7.3 fusion.153
  203.9 7.3 fusion.153
  225.8 7.3 fusion.153
  247.7 7.3 fusion.153
  264.6 12.7 reduce.19
  283.2 11.5 all-to-all-done.1
  326.2 159.5 %reduce-scatter.24.cloned.1.call-done = f32[3072,96]{0,1:T(8,128)} async-done(((f32[3072,768]{0,1:T(8,128)}), f32[3072,96]{0,1:T(8,128)}) %reduce-scatter.24.cloned.1.call-update) | async-done | bytes 1179664 | tf_op jit(solution)/shard_map/reduce_scatter | solution.py:270
  488.0 21.9 %reduce-scatter.26.cloned.1.call-done = bf16[768,96]{0,1:T(8,128)(2,1)} async-done(((bf16[3072,96]{0,1:T(8,128)(2,1)}), bf16[768,96]{0,1:T(8,128)(2,1)}) %reduce-scatter.26.cloned.1.call-update) | async-done | bytes 147472 | tf_op jit(solution)/shard_map/reduce_scatter | solution.py:283
  512.5 41.3 %all-gather.16.cloned.1.call-done = bf16[768,768]{0,1:T(8,128)(2,1)} async-done(((bf16[768,96]{0,1:T(8,128)(2,1)}), bf16[768,768]{0,1:T(8,128)(2,1)}) %all-gather.16.cloned.1.call-update) | async-done | bytes 1179664 | tf_op jit(solution)/shard_map/all_gather | solution.py:174
  562.4 52.1 %collective-permute-done.1 = bf16[1536,768]{0,1:T(8,128)(2,1)} collective-permute-done((bf16[1536,768]{0,1:T(8,128)(2,1)}, bf16[1536,768]{0,1:T(8,128)(2,1)}, u32[]{:S(2)}, u32[]{:S(2)}) %collective-permute-start.1) | collective-permute-done | bytes 2359328 | tf_op jit(solution)/shard_map/ppermute | solution.py:22
  614.5 12.9 convert_reduce_fusion
  647.5 7.8 all-to-all-done.2
  659.6 139.0 %while.47 = (s32[]{:T(128)}, f32[3,2048,64]{1,2,0:T(8,128)}, f32[3,2048,64]{1,2,0:T(8,128)}, bf16[4,3,512,64]{2,3,1,0:T(8,128)(2,1)}, s32[4]{0:T(128)S(1)}, /*in...) while((s32[]{:T(128)}, f32[3,2048,64]{1,2,0:T(8,128)}, ...), condition=%wide.region_12.13_spmd.clone, body=%wide.region_10.12_spmd.clone.sunk | while | flops 2063563776 | bytes 219593376 | solution.py:124
  665.4 7.3 multiply_reduce_fusion.5
  699.9 7.3 multiply_reduce_fusion.5
  734.6 7.3 multiply_reduce_fusion.5
  769.3 7.3 multiply_reduce_fusion.5
  807.7 53.9 %all_to_all.60 = bf16[1,2048,3,1,192]{4,2,3,0,1:T(4,128)(2,1)} all-to-all(bf16[1,2048,3,1,192]{4,2,3,0,1:T(4,128)(2,1)} %copy.188), channel_id=1, replica_groups=mesh['dp'=8,'seq'=4] {'seq'}, dimensions={1} | all-to-all | bytes 4718592 | tf_op jit(solution)/shard_map/all_to_all | solution.py:240
  861.6 7.2 copy.209
  876.7 8.9 fusion.93
  901.2 101.9 %reduce-scatter.16.cloned.1.call-done = f32[768,288]{0,1:T(8,128)} async-done(((f32[768,2304]{0,1:T(8,128)}), f32[768,288]{0,1:T(8,128)}) %reduce-scatter.16.cloned.1.call-update) | async-done | bytes 884752 | tf_op jit(solution)/shard_map/reduce_scatter | solution.py:267
  1005.5 10.7 fusion.63
  1016.2 153.2 %reduce-scatter.20.cloned.1.call-done = f32[768,384]{1,0:T(8,128)} async-done(((f32[768,3072]{1,0:T(8,128)}), f32[768,384]{1,0:T(8,128)}) %reduce-scatter.20.cloned.1.call-update) | async-done | bytes 1179664 | tf_op jit(solution)/shard_map/reduce_scatter | solution.py:269
  1174.8 58.7 %reduce-scatter.32.cloned.1.call-done = f32[96,12]{1,0:T(8,128)} async-done(((f32[768,12]{1,0:T(8,128)}), f32[96,12]{1,0:T(8,128)}) %reduce-scatter.32.cloned.1.call-update) | async-done | bytes 4624
  1241.3 14.0 %reduce-scatter.30.cloned.1.call-done = bf16[192,96]{1,0:T(8,128)(2,1)} async-done(((bf16[768,96]{1,0:T(8,128)(2,1)}), bf16[192,96]{1,0:T(8,128)(2,1)}) %reduce-scatter.30.cloned.1.call-update) | async-done | bytes 36880
  1260.2 19.9 %reduce-scatter.28.cloned.1.call-done = bf16[192,288]{1,0:T(8,128)(2,1)} async-done(((bf16[768,288]{1,0:T(8,128)(2,1)}), bf16[192,288]{1,0:T(8,128)(2,1)}) %reduce-scatter.28.cloned.1.call-update) | async-done | bytes 110608
  1285.7 18.9 %reduce-scatter.22.cloned.1.call-done = bf16[192,384]{1,0:T(8,128)(2,1)} async-done(((bf16[768,384]{1,0:T(8,128)(2,1)}), bf16[192,384]{1,0:T(8,128)(2,1)}) %reduce-scatter.22.cloned.1.call-update) | async-done | bytes 147472 | tf_op jit(solution)/shard_map/reduce_scatter | solution.py:280
  (453 shorter events, 344.6 us)
Async XLA Ops:
  7.2 99.6 %all-gather.8.cloned.1.call-start = ((), (), s32[]{:S(2)}) async-start(), calls=%async_computation.13 | async-start | bytes 4423680 | tf_op jit(solution)/shard_map/all_gather | solution.py:178
  44.5 61.1 %copy-start.9 = (bf16[1,512,768]{2,1,0:T(8,128)(2,1)S(1)}, bf16[1,512,768]{2,1,0:T(8,128)(2,1)}, u32[]{:S(2)}) copy-start(bf16[1,512,768]{2,1,0:T(8,128)(2,1)} %param.21) | copy-start | bytes 2359300
  45.8 75.4 %all-gather.12.cloned.1.call-start = ((), (), s32[]{:S(2)}) async-start(), calls=%async_computation.15 | async-start | bytes 1327104 | tf_op jit(solution)/shard_map/all_gather | solution.py:173
  46.6 261.9 %all-gather.10.cloned.1.call-start = ((), (), s32[]{:S(2)}) async-start(), calls=%async_computation.14 | async-start | bytes 1474560 | tf_op jit(solution)/shard_map/all_gather | solution.py:179
  117.5 38.4 %all-to-all-start = ((bf16[1,512,3,4,192]{1,4,2,0,3:T(8,128)(2,1)}), bf16[1,512,3,4,192]{1,4,2,0,3:T(8,128)(2,1)S(1)}, u32[]{:S(2)}, u32[]{:S(2)}) async-start(bf16[1,512,3,4,192]{1,4,2,0,3:T(8,128)(2,1)} %copy.176), calls=%async_computation | async-start | bytes 4718592 | tf_op jit(solution)/shard_map/all_to_all | solution.py:192
  121.1 191.4 %all-gather.14.cloned.1.call-start = ((), (), s32[]{:S(2)}) async-start(), calls=%async_computation.16 | async-start | bytes 5898240 | tf_op jit(solution)/shard_map/all_gather | solution.py:180
  279.7 15.1 %all-to-all-start.1 = ((bf16[4,2,49152]{2,1,0:T(2,128)(2,1)}), bf16[4,2,49152]{2,1,0:T(2,128)(2,1)S(1)}, u32[]{:S(2)}, u32[]{:S(2)}) async-start(bf16[4,2,49152]{2,1,0:T(2,128)(2,1)} %reshape.401), calls=%async_computation.1 | async-start | bytes 1572864 | tf_op jit(solution)/shard_map/all_to_all | solution.py:201
  283.2 202.6 %reduce-scatter.24.cloned.1.call-start = ((), (), s32[]{:S(2)}) async-start(), calls=%async_computation.22 | async-start | bytes 10616832 | tf_op jit(solution)/shard_map/reduce_scatter | solution.py:270
  283.2 331.3 %copy-start.55 = (f32[3072]{0:T(1024)}, f32[3072]{0:T(1024)S(1)}, u32[]{:S(2)}) copy-start(f32[3072]{0:T(1024)S(1)} %add.276) | copy-start | bytes 36868
  311.0 323.4 %copy-start.46 = (f32[512]{0:T(512)}, f32[512]{0:T(512)S(1)}, u32[]{:S(2)}) copy-start(f32[512]{0:T(512)S(1)} %broadcast_multiply_fusion) | copy-start | bytes 6148
  312.5 322.0 %copy-start.58 = (f32[512]{0:T(512)}, f32[512]{0:T(512)S(1)}, u32[]{:S(2)}) copy-start(f32[512]{0:T(512)S(1)} %fusion.87) | copy-start | bytes 6148
  326.2 183.7 %reduce-scatter.26.cloned.1.call-start = ((), (), s32[]{:S(2)}) async-start(), calls=%async_computation.23 | async-start | bytes 737280 | tf_op jit(solution)/shard_map/reduce_scatter | solution.py:283
  487.9 65.8 %all-gather.16.cloned.1.call-start = ((), (), s32[]{:S(2)}) async-start(), calls=%async_computation.17 | async-start | bytes 1327104 | tf_op jit(solution)/shard_map/all_gather | solution.py:174
  553.7 3.2 collective-permute-start
  560.9 53.6 %collective-permute-start.1 = (bf16[1536,768]{0,1:T(8,128)(2,1)}, bf16[1536,768]{0,1:T(8,128)(2,1)}, u32[]{:S(2)}, u32[]{:S(2)}) collective-permute-start(bf16[1536,768]{0,1:T(8,128)(2,1)} %maximum_select_fusion.1), channel_id=1, source_target_pairs={{0,2},{1,3},{2,0},{3,1},{4,6},{5,7},{6,4},{7,5},{8,10},{9,11},{10,... | collective-permute-start | bytes 7077896 | tf_op jit(solution)/shard_map/ppermute | solution.py:22
  562.4 65.0 %copy-start.15 = (f32[512,768]{1,0:T(8,128)S(1)}, f32[512,768]{1,0:T(8,128)}, u32[]{:S(2)}) copy-start(f32[512,768]{1,0:T(8,128)} %copy-done.14) | copy-start | bytes 4718596
  640.2 15.1 %all-to-all-start.2 = ((bf16[1,512,4,192]{1,3,0,2:T(8,128)(2,1)}), bf16[1,512,4,192]{1,3,0,2:T(8,128)(2,1)S(1)}, u32[]{:S(2)}, u32[]{:S(2)}) async-start(bf16[1,512,4,192]{1,3,0,2:T(8,128)(2,1)} %bitcast.198), calls=%async_computation.2 | async-start | bytes 1572864 | tf_op jit(solution)/shard_map/all_to_all | solution.py:229
  643.7 251.1 %reduce-scatter.18.cloned.1.call-start = ((), (), s32[]{:S(2)}) async-start(), calls=%async_computation.19 | async-start | bytes 2654208 | tf_op jit(solution)/shard_map/reduce_scatter | solution.py:268
  647.5 355.6 %reduce-scatter.16.cloned.1.call-start = ((), (), s32[]{:S(2)}) async-start(), calls=%async_computation.18 | async-start | bytes 7962624 | tf_op jit(solution)/shard_map/reduce_scatter | solution.py:267
  876.0 293.4 %reduce-scatter.20.cloned.1.call-start = ((), (), s32[]{:S(2)}) async-start(), calls=%async_computation.20 | async-start | bytes 10616832 | tf_op jit(solution)/shard_map/reduce_scatter | solution.py:269
  885.7 347.8 %reduce-scatter.32.cloned.1.call-start = ((), (), s32[]{:S(2)}) async-start(), calls=%async_computation.26 | async-start | bytes 442368
  894.8 360.5 %reduce-scatter.30.cloned.1.call-start = ((), (), s32[]{:S(2)}) async-start(), calls=%async_computation.25 | async-start | bytes 245760
  896.7 108.8 %copy-start.16 = (f32[512,768]{1,0:T(8,128)S(1)}, f32[512,768]{1,0:T(8,128)}, u32[]{:S(2)}) copy-start(f32[512,768]{1,0:T(8,128)} %copy-done.14) | copy-start | bytes 4718596
  896.7 108.8 %copy-start.56 = (f32[3072]{0:T(1024)S(1)}, f32[3072]{0:T(1024)}, u32[]{:S(2)}) copy-start(f32[3072]{0:T(1024)} %copy-done.55) | copy-start | bytes 36868
  896.7 108.8 %copy-start.61 = (f32[768]{0:T(1024)S(1)}, f32[768]{0:T(1024)}, u32[]{:S(2)}) copy-start(f32[768]{0:T(1024)} %get-tuple-element.359) | copy-start | bytes 9220
  896.7 383.3 %reduce-scatter.28.cloned.1.call-start = ((), (), s32[]{:S(2)}) async-start(), calls=%async_computation.24 | async-start | bytes 737280
  1005.4 299.3 %reduce-scatter.22.cloned.1.call-start = ((), (), s32[]{:S(2)}) async-start(), calls=%async_computation.21 | async-start | bytes 737280 | tf_op jit(solution)/shard_map/reduce_scatter | solution.py:280
  1016.2 155.5 %copy-start.8 = (f32[512,768]{1,0:T(8,128)S(1)}, f32[512,768]{1,0:T(8,128)}, u32[]{:S(2)}) copy-start(f32[512,768]{1,0:T(8,128)} %copy-done.7) | copy-start | bytes 4718596
  1016.2 155.5 %copy-start.19 = (bf16[1,512,768]{2,1,0:T(8,128)(2,1)S(1)}, bf16[1,512,768]{2,1,0:T(8,128)(2,1)}, u32[]{:S(2)}) copy-start(bf16[1,512,768]{2,1,0:T(8,128)(2,1)} %param.22) | copy-start | bytes 2359300
  1171.7 84.5 %copy-start.29 = (f32[192,96]{0,1:T(8,128)S(1)}, f32[192,96]{0,1:T(8,128)}, u32[]{:S(2)}) copy-start(f32[192,96]{0,1:T(8,128)} %copy-done.28) | copy-start | bytes 221188
  1171.7 109.4 %copy-start.22 = (f32[192,288]{0,1:T(8,128)S(1)}, f32[192,288]{0,1:T(8,128)}, u32[]{:S(2)}) copy-start(f32[192,288]{0,1:T(8,128)} %copy-done.21) | copy-start | bytes 663556
  1258.7 45.9 %copy-start.35 = (f32[192,384]{1,0:T(8,128)S(1)}, f32[192,384]{1,0:T(8,128)}, u32[]{:S(2)}) copy-start(f32[192,384]{1,0:T(8,128)} %param.30) | copy-start | bytes 884740
  (105 other events, 619.0 us)
Sparse Core Ops, SparseCore 0:
  45.9 31.3 all-gather.7
  79.9 40.8 all-gather.11
  123.0 22.7 all-gather.9
  147.2 37.4 all-gather.13
  326.3 159.4 reduce-scatter.23
  488.7 21.1 reduce-scatter.25
  512.7 41.0 all-gather.15
  648.1 68.2 reduce-scatter.17
  876.2 126.8 reduce-scatter.15
  1006.9 162.4 reduce-scatter.19
  1173.0 60.3 reduce-scatter.31
  1236.5 18.7 reduce-scatter.29
  1258.0 22.0 reduce-scatter.27
  1282.6 22.0 reduce-scatter.21
